TPU v7x, 32 devices: a whole 2x2x4 slice. The times are simulated.
32 devices in a mesh: mom: 2 (over x), pts: 16 (over z, y, core).
Axes of the slice: x: 2, y: 2, z: 4, core: 2. Of those that a mesh axis runs over, the one named last changes fastest.
Arguments:
- amplitudes: bfloat16 [2, 2, 1, 256, 64, 128], P(None, None, None, 'mom'), may hold values from -6 to 6
- val_orbitals: bfloat16 [2, 256, 64, 512], P(None, 'mom'), may hold values from -0.25 to 0.25
- cond_orbitals: bfloat16 [2, 256, 512, 128], P(None, 'mom', 'pts'), may hold values from -0.25 to 0.25
- screened: bfloat16 [2, 256, 512, 512], P(None, None, ('pts', 'mom')), may hold values from -12 to 12
- val_energy: float32 [256, 64], P('mom', 'pts'), may hold values from -2 to -0.5
- cond_energy: float32 [256, 128], P('mom'), may hold values from 0.5 to 2
- grid_of_slot: int32 [256], replicated, may hold values from 0 to 255, as said below
- opposite_slot: int32 [256], P('mom'), may hold values from 0 to 255, as said below
Outputs:
- applied: float32 [2, 2, 1, 256, 64, 128], P(None, None, None, 'mom', 'pts')
Inputs may be any that keep to these rules, and one draw needn't show every extreme that they name: `grid_of_slot`: a permutation of the grid indices. opposite_slot[s] is the slot whose grid index is 255 - grid_of_slot[s]; it is never s, and s and opposite_slot[s] lie in aligned blocks of 128 slots whose first slots differ by 128.
All inputs are finite; a program needn't handle non-finite values.
Results may differ from a plain program's by a relative error of at most 0.006.
Values may be sent and summed in bfloat16 or wider, within the bound.
No kernel may reach another device: no remote copies, remote signals or barrier semaphores. Data moves between devices by JAX's collectives and lax.ppermute only.
A program may use at most 256 MiB of HBM per device.

v0:
```python
import math
import jax
import jax.numpy as jnp
from jax import lax
from jax.sharding import PartitionSpec as P


def partner_2(value, axis, apart):
    mask = 2**apart
    pairs = [(source, source ^ mask) for source in range(lax.axis_size(axis))]
    return lax.ppermute(value, axis, pairs)


def complex_mix(formula, left, right, left_sign, right_sign):
    real_real = jnp.einsum(formula, left[0], right[0], preferred_element_type=jnp.float32)
    imag_imag = jnp.einsum(formula, left[1], right[1], preferred_element_type=jnp.float32)
    real_imag = jnp.einsum(formula, left[0], right[1], preferred_element_type=jnp.float32)
    imag_real = jnp.einsum(formula, left[1], right[0], preferred_element_type=jnp.float32)
    return jnp.stack(
        [
            real_real - left_sign * right_sign * imag_imag,
            right_sign * real_imag + left_sign * imag_real,
        ]
    )


def on_device(
    amplitudes,
    val_orbitals,
    cond_orbitals,
    screened,
    val_energy,
    cond_energy,
    grid_of_slot,
    opposite_slot,
):
    slots_here = opposite_slot.shape[0]
    total_slots = grid_of_slot.shape[0]
    rows_here = val_energy.shape[1]
    frequency = jnp.arange(total_slots, dtype=jnp.int32)
    phases = frequency[:, None] * grid_of_slot[None, :] % total_slots
    angles = phases.astype(jnp.float32) * (2.0 * math.pi / total_slots)
    cosine_table = jnp.cos(angles).astype(jnp.bfloat16)
    sine_table = jnp.sin(angles).astype(jnp.bfloat16)
    half_product = complex_mix("bnkvc,kuc->bnkvu", amplitudes, cond_orbitals, 1.0, 1.0).astype(
        jnp.bfloat16
    )
    pair_values = complex_mix("bnkvu,kvm->bnkum", half_product, val_orbitals, 1.0, -1.0).astype(
        jnp.bfloat16
    )
    flattened = pair_values.reshape(pair_values.shape[:4] + (-1,))
    weights = screened.reshape(2, total_slots, -1)
    inverse_count = 1.0 / total_slots
    whole_k = lax.all_to_all(flattened, "mom", split_axis=4, concat_axis=3, tiled=True)
    spec_real = jnp.einsum(
        "fs,bnsc->bnfc", cosine_table, whole_k[0], preferred_element_type=jnp.float32
    ) + jnp.einsum("fs,bnsc->bnfc", sine_table, whole_k[1], preferred_element_type=jnp.float32)
    spec_imag = jnp.einsum(
        "fs,bnsc->bnfc", cosine_table, whole_k[1], preferred_element_type=jnp.float32
    ) - jnp.einsum("fs,bnsc->bnfc", sine_table, whole_k[0], preferred_element_type=jnp.float32)
    prod_real = (weights[0] * spec_real - weights[1] * spec_imag).astype(jnp.bfloat16)
    prod_imag = (weights[0] * spec_imag + weights[1] * spec_real).astype(jnp.bfloat16)
    back_real = (
        jnp.einsum("fs,bnfc->bnsc", cosine_table, prod_real, preferred_element_type=jnp.float32)
        - jnp.einsum("fs,bnfc->bnsc", sine_table, prod_imag, preferred_element_type=jnp.float32)
    ) * inverse_count
    back_imag = (
        jnp.einsum("fs,bnfc->bnsc", cosine_table, prod_imag, preferred_element_type=jnp.float32)
        + jnp.einsum("fs,bnfc->bnsc", sine_table, prod_real, preferred_element_type=jnp.float32)
    ) * inverse_count
    field_pts = lax.all_to_all(
        jnp.stack([back_real, back_imag]).astype(jnp.bfloat16),
        "mom",
        split_axis=3,
        concat_axis=4,
        tiled=True,
    )
    field_pts = field_pts.reshape(pair_values.shape)
    weighted = complex_mix("bnkum,kvm->bnkvu", field_pts, val_orbitals, 1.0, 1.0).astype(
        jnp.bfloat16
    )
    rows_mine = lax.all_to_all(weighted, "pts", split_axis=4, concat_axis=5, tiled=True)
    band_values = complex_mix(
        "bnkvu,kuc->bnkvc",
        rows_mine,
        lax.all_gather(cond_orbitals, "pts", axis=2, tiled=True),
        1.0,
        -1.0,
    )
    top_bit = lax.axis_size("mom").bit_length() - 2
    partner = partner_2(band_values.astype(jnp.bfloat16), "mom", top_bit).astype(band_values.dtype)
    mirrored = jnp.take(partner, opposite_slot % slots_here, axis=3)
    start_row = lax.axis_index("pts") * rows_here
    own_rows = lax.dynamic_slice_in_dim(amplitudes, start_row, rows_here, 4).astype(jnp.float32)
    energy_gap = cond_energy[:, None, :] - val_energy[:, :, None]
    result_real = energy_gap * own_rows[0, 0] - band_values[0, 0] - mirrored[0, 1]
    result_imag = energy_gap * own_rows[1, 0] - band_values[1, 0] + mirrored[1, 1]
    anti_real = -energy_gap * own_rows[0, 1] + band_values[0, 1] + mirrored[0, 0]
    anti_imag = -energy_gap * own_rows[1, 1] + band_values[1, 1] - mirrored[1, 0]
    return jnp.stack([jnp.stack([result_real, anti_real]), jnp.stack([result_imag, anti_imag])])


def solution(mesh):
    in_specs = (
        P(None, None, None, "mom", None, None),
        P(None, "mom", None, None),
        P(None, "mom", "pts", None),
        P(None, None, ("pts", "mom"), None),
        P("mom", "pts"),
        P("mom", None),
        P(),
        P("mom"),
    )
    out_specs = P(None, None, None, "mom", "pts", None)
    return jax.shard_map(
        on_device, mesh=mesh, in_specs=in_specs, out_specs=out_specs, check_vma=False
    )
```

profile of v0, /device:TPU:0, one launch (start us, length us, event | category | flops | bytes accessed | tf_op | source)
XLA Modules:
  0.0 1007.6 jit_solution(14866260467784046337)
XLA Ops:
  7.3 4.6 fusion.134
  11.9 4.1 fusion.41
  16.0 4.1 fusion.40
  20.1 5.4 fusion.44
  25.5 5.4 fusion.45
  30.9 9.8 fusion.17
  40.7 14.0 %fusion.34 = bf16[2,1,128,32,512]{4,3,0,2,1:T(8,128)(2,1)} fusion(f32[128,2,32,512]{3,2,1,0:T(8,128)} %fusion.17, bf16[2,128,64,32]{2,3,0,1:T(8,128)(2,1)} %fusion.45, bf16[2,128,64,512]{3,2,1,0:T(8,128)(2,1)} %param.9), kind=kOutput, calls=%fused_computation.51 | convolution fusion | flops 549453824 | bytes 35651584 | tf_op jit(solution)/shard_map/bnkvu,kvm->bnkum/dot_general | solution.py:16
  54.7 16.5 %copy.203 = bf16[2,1,128,32,512]{2,0,4,3,1:T(2,128)(2,1)} copy(bf16[2,1,128,32,512]{4,3,0,2,1:T(8,128)(2,1)} %fusion.34) | data formatting | bytes 16777216 | tf_op jit(solution)/shard_map/stack | solution.py:19
  71.2 12.1 %fusion.23 = f32[128,2,32,512]{3,2,1,0:T(8,128)} fusion(bf16[2,128,64,32]{2,3,0,1:T(8,128)(2,1)S(1)} %copy-done.4, bf16[2,128,64,512]{3,2,1,0:T(8,128)(2,1)} %param.9), kind=kOutput, calls=%fused_computation.40 | convolution fusion | flops 536870912 | bytes 26214400 | tf_op jit(solution)/shard_map/bnkvu,kvm->bnkum/dot_general | solution.py:17
  83.4 12.9 %fusion.37 = bf16[2,1,128,32,512]{4,3,0,2,1:T(8,128)(2,1)} fusion(bf16[2,128,64,32]{2,3,0,1:T(8,128)(2,1)S(1)} %copy-done.2, bf16[2,128,64,512]{3,2,1,0:T(8,128)(2,1)} %param.9, f32[128,2,32,512]{3,2,1,0:T(8,128)} %fusion.23), kind=kOutput, calls=%fused_computation.52 | convolution fusion | flops 549453824 | bytes 34603008 | tf_op jit(solution)/shard_map/bnkvu,kvm->bnkum/dot_general | solution.py:18
  96.3 15.7 %copy.204 = bf16[2,1,128,32,512]{2,0,4,3,1:T(2,128)(2,1)} copy(bf16[2,1,128,32,512]{4,3,0,2,1:T(8,128)(2,1)} %fusion.37) | data formatting | bytes 16777216 | tf_op jit(solution)/shard_map/stack | solution.py:19
  112.0 26.4 %pad_maximum_fusion = bf16[2,2,1,128,16384]{3,1,2,0,4:T(2,128)(2,1)} fusion(bf16[1,2,1,128,16384]{3,1,2,0,4:T(2,128)(2,1)} %bitcast.316, bf16[1,2,1,128,16384]{3,1,2,0,4:T(2,128)(2,1)} %bitcast.315), kind=kLoop, calls=%fused_computation.3 | loop fusion | flops 8388608 | bytes 33554432 | tf_op jit(solution)/shard_map/stack | solution.py:19
  138.4 9.8 all-to-all-start
  148.2 12.1 %slice_convert_fusion.1 = (f32[1,256,16,512]{3,2,1,0:T(8,128)}, f32[1,256,16,512]{3,2,1,0:T(8,128)}) fusion(bf16[2,256,16,512]{3,2,1,0:T(8,128)(2,1)} %param.11), kind=kLoop, calls=%fused_computation.61 | loop fusion | flops 4194304 | bytes 25165824 | tf_op jit(solution)/shard_map/convert_element_type | solution.py:61
  160.3 9.9 copy.202
  170.2 10.0 copy.205
  180.2 150.9 %all-to-all-done = bf16[2,2,1,128,16384]{3,1,2,0,4:T(2,128)(2,1)} async-done(((bf16[2,2,1,128,16384]{3,1,2,0,4:T(2,128)(2,1)}), bf16[2,2,1,128,16384]{3,1,2,0,4:T(2,128)(2,1)}, u32[]{:S(2)}, u32[]{:S(2)}) %all-to-all-start) | async-done | bytes 16777248 | tf_op jit(solution)/shard_map/all_to_all | solution.py:54
  331.1 28.1 %copy.246 = bf16[2,2,1,128,2,8192]{3,4,5,1,2,0:T(2,128)(2,1)S(1)} copy(bf16[2,2,1,128,2,8192]{3,1,0,5,4,2:T(2,128)(2,1)} %bitcast.38) | data formatting | bytes 33554432 | tf_op jit(solution)/shard_map/all_to_all | solution.py:54
  359.2 13.0 %fusion.133 = (bf16[1,2,1,2,128,8192]{4,3,5,1,2,0:T(2,128)(2,1)}, bf16[1,2,1,2,128,8192]{4,3,5,1,2,0:T(2,128)(2,1)}) fusion(bf16[2,2,1,2,128,8192]{4,3,5,1,2,0:T(2,128)(2,1)S(1)} %bitcast.312), kind=kLoop, calls=%fused_computation.179 | loop fusion | bytes 33554432 | tf_op jit(solution)/shard_map/slice | solution.py:57
  372.2 14.1 %reshape.539 = bf16[2,256,8192]{1,2,0:T(8,128)(2,1)} reshape(bf16[1,2,1,2,128,8192]{4,3,5,1,2,0:T(2,128)(2,1)} %get-tuple-element.15) | data formatting | bytes 16777216 | tf_op jit(solution)/shard_map/reshape.28
  386.3 14.2 %reshape.538 = bf16[2,256,8192]{1,2,0:T(8,128)(2,1)} reshape(bf16[1,2,1,2,128,8192]{4,3,5,1,2,0:T(2,128)(2,1)} %get-tuple-element.16) | data formatting | bytes 16777216 | tf_op jit(solution)/shard_map/reshape.24
  400.5 12.5 %fusion.91 = f32[2,8192,256]{2,1,0:T(8,128)} fusion(bf16[2,256,8192]{1,2,0:T(8,128)(2,1)} %reshape.539, s32[256]{0:T(256)S(1)} %copy-done.6), kind=kOutput, calls=%fused_computation.134 | convolution fusion | flops 2148466688 | bytes 25166848 | tf_op jit(solution)/shard_map/fs,bnsc->bnfc/dot_general | solution.py:58
  413.1 9.0 fusion.93
  422.1 14.8 %convolution_subtract_fusion = f32[2,8192,256]{2,1,0:T(8,128)} fusion(f32[2,8192,256]{2,1,0:T(8,128)} %fusion.91, bf16[2,256,8192]{1,2,0:T(8,128)(2,1)S(1)} %copy-done.1, s32[256]{0:T(256)S(1)} %copy-done.6), kind=kOutput, calls=%fused_computation.23 | convolution fusion | flops 2152660992 | bytes 41944064 | tf_op jit(solution)/shard_map/fs,bnsc->bnfc/dot_general | solution.py:60
  436.9 27.2 %fusion.11 = (bf16[2,256,8192]{1,2,0:T(8,128)(2,1)}, bf16[2,256,8192]{1,2,0:T(8,128)(2,1)}) fusion(f32[2,8192,256]{2,1,0:T(8,128)} %convolution_subtract_fusion, f32[256,8192]{0,1:T(8,128)} %bitcast.311, f32[256,8192]{0,1:T(8,128)} %bitcast.310, f32[2,8192,256]{2,1,0:T(8,128)} %fusion.93, bf16[2,256,8192]{1,2,0:T(8,128)(2,1)} %reshape.539, s32[256]{0:T(256)S(1)} %copy-done.6), kind=kOutput, calls=%fused_computation.28 | convolution fusion | flops 2186215424 | bytes 75498496 | tf_op jit(solution)/shard_map/fs,bnsc->bnfc/dot_general | solution.py:57
  464.1 12.5 %fusion.89 = f32[2,8192,256]{2,1,0:T(8,128)} fusion(bf16[2,256,8192]{1,2,0:T(8,128)(2,1)} %get-tuple-element.11, s32[256]{0:T(256)S(1)} %copy-done.6), kind=kOutput, calls=%fused_computation.133 | convolution fusion | flops 2148466688 | bytes 25166848 | tf_op jit(solution)/shard_map/fs,bnfc->bnsc/dot_general | solution.py:64
  476.7 9.0 fusion.87
  485.7 13.5 %fusion.8 = bf16[1,2,1,256,8192]{3,4,1,2,0:T(8,128)(2,1)} fusion(f32[2,8192,256]{2,1,0:T(8,128)} %fusion.89, bf16[2,256,8192]{1,2,0:T(8,128)(2,1)} %get-tuple-element.12, s32[256]{0:T(256)S(1)} %copy-done.6), kind=kOutput, calls=%fused_computation.25 | convolution fusion | flops 2161049600 | bytes 33555456 | tf_op jit(solution)/shard_map/fs,bnfc->bnsc/dot_general | solution.py:65
  499.2 11.5 %fusion.9 = bf16[1,2,1,256,8192]{3,4,1,2,0:T(8,128)(2,1)} fusion(f32[2,8192,256]{2,1,0:T(8,128)} %fusion.87, bf16[2,256,8192]{1,2,0:T(8,128)(2,1)S(1)} %bitcast.309, s32[256]{0:T(256)S(1)} %copy-done.6), kind=kOutput, calls=%fused_computation.26 | convolution fusion | flops 2161049600 | bytes 33555456 | tf_op jit(solution)/shard_map/fs,bnfc->bnsc/dot_general | solution.py:69
  510.8 13.7 %pad_maximum_fusion.1 = bf16[2,2,1,256,8192]{3,4,1,2,0:T(8,128)(2,1)} fusion(bf16[1,2,1,256,8192]{3,4,1,2,0:T(8,128)(2,1)} %fusion.9, bf16[1,2,1,256,8192]{3,4,1,2,0:T(8,128)(2,1)} %fusion.8), kind=kLoop, calls=%fused_computation.4 | loop fusion | flops 8388608 | bytes 33554432 | tf_op jit(solution)/shard_map/stack | solution.py:72
  524.5 41.2 %copy.175 = bf16[2,2,1,256,8192]{4,1,2,0,3:T(2,128)(2,1)} copy(bf16[2,2,1,256,8192]{3,4,1,2,0:T(8,128)(2,1)} %pad_maximum_fusion.1) | data formatting | bytes 33554432 | tf_op jit(solution)/shard_map/stack | solution.py:72
  565.7 200.1 %all_to_all.45 = bf16[2,2,1,256,8192]{4,1,2,0,3:T(2,128)(2,1)} all-to-all(bf16[2,2,1,256,8192]{4,1,2,0,3:T(2,128)(2,1)} %copy.175), channel_id=1, replica_groups=mesh['mom'=2,'pts'=16] {'mom'}, dimensions={3} | all-to-all | bytes 33554432 | tf_op jit(solution)/shard_map/all_to_all | solution.py:71
  765.8 30.2 %copy.245 = bf16[2,2,1,2,128,8192]{5,3,1,4,2,0:T(2,128)(2,1)S(1)} copy(bf16[2,2,1,2,128,8192]{5,1,0,4,3,2:T(2,128)(2,1)} %bitcast.314) | data formatting | bytes 33554432 | tf_op jit(solution)/shard_map/all_to_all | solution.py:71
  796.1 14.9 %fusion.132 = (bf16[1,2,1,128,2,8192]{5,4,1,3,2,0:T(2,128)(2,1)}, bf16[1,2,1,128,2,8192]{5,4,1,3,2,0:T(2,128)(2,1)}) fusion(bf16[2,2,1,128,2,8192]{5,4,1,3,2,0:T(2,128)(2,1)S(1)} %bitcast.313), kind=kLoop, calls=%fused_computation.178 | loop fusion | bytes 33554432 | tf_op jit(solution)/shard_map/slice | solution.py:15
  811.0 14.3 %reshape.542 = bf16[2,128,32,512]{3,2,0,1:T(8,128)(2,1)} reshape(bf16[1,2,1,128,2,8192]{5,4,1,3,2,0:T(2,128)(2,1)} %get-tuple-element.13) | data formatting | bytes 16777216 | tf_op jit(solution)/shard_map/reshape.50
  825.2 14.3 %reshape.543 = bf16[2,128,32,512]{3,2,0,1:T(8,128)(2,1)} reshape(bf16[1,2,1,128,2,8192]{5,4,1,3,2,0:T(2,128)(2,1)} %get-tuple-element.14) | data formatting | bytes 16777216 | tf_op jit(solution)/shard_map/reshape.54
  839.5 10.1 fusion.14
  849.6 10.1 fusion.12
  859.6 9.3 fusion.46
  868.9 10.7 %fusion.47 = bf16[1,2,1,128,64,32]{4,5,1,3,2,0:T(8,128)(2,1)} fusion(f32[128,2,32,64]{3,2,1,0:T(8,128)} %fusion.12, bf16[2,128,32,512]{3,2,0,1:T(8,128)(2,1)} %reshape.542, bf16[2,128,64,512]{3,2,1,0:T(8,128)(2,1)} %param.9), kind=kOutput, calls=%fused_computation.69 | convolution fusion | flops 537919488 | bytes 22020096 | tf_op jit(solution)/shard_map/bnkum,kvm->bnkvu/dot_general | solution.py:17
  879.6 4.6 pad_maximum_fusion.2
  884.2 8.0 copy.177
  892.1 52.0 %all_to_all.46 = bf16[2,2,1,128,64,32]{3,5,2,1,0,4:T(8,128)(2,1)S(1)} all-to-all(bf16[2,2,1,128,64,32]{3,5,2,1,0,4:T(8,128)(2,1)S(1)} %copy.177), channel_id=1, replica_groups=mesh['mom'=2,'pts'=16] {'pts'}, dimensions={4} | all-to-all | bytes 4194304 | tf_op jit(solution)/shard_map/all_to_all | solution.py:82
  949.2 7.0 fusion.5
  956.3 7.1 fusion.6
  963.3 7.0 fusion.4
  970.4 7.1 fusion.7
  980.9 12.8 %collective-permute-done = bf16[2,2,1,128,4,128]{5,3,4,2,1,0:T(8,128)(2,1)S(1)} collective-permute-done((bf16[2,2,1,128,4,128]{5,3,4,2,1,0:T(8,128)(2,1)S(1)}, bf16[2,2,1,128,4,128]{5,3,4,2,1,0:T(8,128)(2,1)S(1)}, u32[]{:S(2)}, u32[]{:S(2)}) %collective-permute-start) | collective-permute-done | bytes 524320 | tf_op jit(solution)/shard_map/ppermute | solution.py:11
  (58 shorter events, 16.0 us)
Async XLA Ops:
  6.5 942.7 %all-gather.2.cloned.1.call-start = ((), (), s32[]{:S(2)}) async-start(), calls=%async_computation.3 | async-start | bytes 35651584 | tf_op jit(solution)/shard_map/all_gather | solution.py:86
  7.3 4.6 copy-start.3
  16.0 14.9 %slice-start = ((s8[16777216]{0:T(1024)(128)(4,1)}), s8[4194304]{0:T(1024)(128)(4,1)S(1)}, s32[]{:S(2)}) async-start(s8[16777216]{0:T(1024)(128)(4,1)} %bitcast.306), calls=%async_computation.4 | async-start | bytes 8388608
  16.0 14.9 %slice-start.1 = ((s8[16777216]{0:T(1024)(128)(4,1)}), s8[4194304]{0:T(1024)(128)(4,1)S(1)}, s32[]{:S(2)}) async-start(s8[16777216]{0:T(1024)(128)(4,1)} %bitcast.306), calls=%async_computation.5 | async-start | bytes 8388608
  20.0 10.8 %slice-start.2 = ((s8[16777216]{0:T(1024)(128)(4,1)}), s8[4194304]{0:T(1024)(128)(4,1)S(1)}, s32[]{:S(2)}) async-start(s8[16777216]{0:T(1024)(128)(4,1)} %bitcast.306), calls=%async_computation.6 | async-start | bytes 8388608
  25.5 5.4 slice-start.3
  54.7 16.5 %copy-start.4 = (bf16[2,128,64,32]{2,3,0,1:T(8,128)(2,1)S(1)}, bf16[2,128,64,32]{2,3,0,1:T(8,128)(2,1)}, u32[]{:S(2)}) copy-start(bf16[2,128,64,32]{2,3,0,1:T(8,128)(2,1)} %fusion.44) | copy-start | bytes 3145732
  71.2 12.1 %copy-start.2 = (bf16[2,128,64,32]{2,3,0,1:T(8,128)(2,1)S(1)}, bf16[2,128,64,32]{2,3,0,1:T(8,128)(2,1)}, u32[]{:S(2)}) copy-start(bf16[2,128,64,32]{2,3,0,1:T(8,128)(2,1)} %fusion.45) | copy-start | bytes 3145732
  138.4 192.7 %all-to-all-start = ((bf16[2,2,1,128,16384]{3,1,2,0,4:T(2,128)(2,1)}), bf16[2,2,1,128,16384]{3,1,2,0,4:T(2,128)(2,1)}, u32[]{:S(2)}, u32[]{:S(2)}) async-start(bf16[2,2,1,128,16384]{3,1,2,0,4:T(2,128)(2,1)} %pad_maximum_fusion), calls=%async_computation | async-start | bytes 33554432 | tf_op jit(solution)/shard_map/all_to_all | solution.py:54
  386.3 14.2 %copy-start.6 = (s32[256]{0:T(256)S(1)}, s32[256]{0:T(256)}, u32[]{:S(2)}) copy-start(s32[256]{0:T(256)} %param.14) | copy-start | bytes 3076
  400.5 12.6 %copy-start.1 = (bf16[2,256,8192]{1,2,0:T(8,128)(2,1)S(1)}, bf16[2,256,8192]{1,2,0:T(8,128)(2,1)}, u32[]{:S(2)}) copy-start(bf16[2,256,8192]{1,2,0:T(8,128)(2,1)} %reshape.538) | copy-start | bytes 25165828
  464.1 12.6 %copy-start = (bf16[2,256,8192]{1,2,0:T(8,128)(2,1)S(1)}, bf16[2,256,8192]{1,2,0:T(8,128)(2,1)}, u32[]{:S(2)}) copy-start(bf16[2,256,8192]{1,2,0:T(8,128)(2,1)} %get-tuple-element.12) | copy-start | bytes 25165828
  464.1 35.1 %slice-start.4 = ((s8[8388608]{0:T(1024)(128)(4,1)}), s8[4194304]{0:T(1024)(128)(4,1)S(1)}, s32[]{:S(2)}) async-start(s8[8388608]{0:T(1024)(128)(4,1)} %bitcast.308), calls=%async_computation.8 | async-start | bytes 8388608
  476.7 22.5 %slice-start.5 = ((s8[8388608]{0:T(1024)(128)(4,1)}), s8[4194304]{0:T(1024)(128)(4,1)S(1)}, s32[]{:S(2)}) async-start(s8[8388608]{0:T(1024)(128)(4,1)} %bitcast.308), calls=%async_computation.9 | async-start | bytes 8388608
  970.4 8.9 copy-start.8
  977.5 18.9 %copy-start.5 = (f32[128,128]{1,0:T(8,128)S(1)}, f32[128,128]{1,0:T(8,128)}, u32[]{:S(2)}) copy-start(f32[128,128]{1,0:T(8,128)} %param.13) | copy-start | bytes 196612
  977.5 18.9 %copy-start.7 = (f32[128,4]{0,1:T(4,128)S(1)}, f32[128,4]{0,1:T(4,128)}, u32[]{:S(2)}) copy-start(f32[128,4]{0,1:T(4,128)} %param.12) | copy-start | bytes 6148
  978.9 14.9 %collective-permute-start = (bf16[2,2,1,128,4,128]{5,3,4,2,1,0:T(8,128)(2,1)S(1)}, bf16[2,2,1,128,4,128]{5,3,4,2,1,0:T(8,128)(2,1)S(1)}, u32[]{:S(2)}, u32[]{:S(2)}) collective-permute-start(bf16[2,2,1,128,4,128]{5,3,4,2,1,0:T(8,128)(2,1)S(1)} %pad_maximum_fusion.4), channel_id=1, source_target_pairs={{0,16},{16,0},{1,17},{17,1},{2,18},{18,2},{3,19},{19,3},{4,20},{20... | collective-permute-start | bytes 1572872 | tf_op jit(solution)/shard_map/ppermute | solution.py:11
Sparse Core Ops, SparseCore 0:
  8.9 170.7 all-gather.1
where the time goes:
time: 1020 us; the launch traced here: 1010 us
  local copies, waits for them, and re-layouts  259 us (25%)
  blocking collectives  252 us (25%)
  matrix products  246 us (24%)
  waiting for transfers between devices  164 us (16%)
  other arithmetic  61.5 us (6%)
  between operations  13.9 us (1%)
    all_to_all x1, blocking collectives, on_device(): lax.all_to_all(jnp.stack([back_real, back_imag]).astype(jnp.bfloat16), 'm...  200 us
    all_to_all x1, waiting for transfers between devices, on_device(): lax.all_to_all(flattened, 'mom', split_axis=4, concat_axis=3, tiled=True)  151 us
    another operation x6, local copies, waits for them, and re-layouts  58.6 us
    all_to_all x1, blocking collectives, on_device(): lax.all_to_all(weighted, 'pts', split_axis=4, concat_axis=5, tiled=True)  52 us
    another operation x1, local copies, waits for them, and re-layouts, on_device(): jnp.stack([back_real, back_imag]).astype(jnp.bfloat16)  41.2 us
    another operation x3, local copies, waits for them, and re-layouts, complex_mix(): jnp.stack([real_real - left_sign * right_sign * imag_imag, right_sign * r...  40.2 us
    dot_general x4, matrix products, complex_mix(): jnp.einsum(formula, left[1], right[1], preferred_element_type=jnp.float32)  35.8 us
    dot_general x4, matrix products, complex_mix(): jnp.einsum(formula, left[1], right[0], preferred_element_type=jnp.float32)  35.4 us
  transfers between devices with their start and end apart: 3, of which 2 were waited for; matrix products, arithmetic and copies ran while one was open for 53% of the time, Pallas kernels for 0%

commit v1 on v0

--- a/solution.py
+++ b/solution.py
@@ -68,12 +68,20 @@
         jnp.einsum("fs,bnfc->bnsc", cosine_table, prod_imag, preferred_element_type=jnp.float32)
         + jnp.einsum("fs,bnfc->bnsc", sine_table, prod_real, preferred_element_type=jnp.float32)
     ) * inverse_count
-    field_pts = lax.all_to_all(
-        jnp.stack([back_real, back_imag]).astype(jnp.bfloat16),
-        "mom",
-        split_axis=3,
-        concat_axis=4,
-        tiled=True,
+    field_pts = jnp.concatenate(
+        lax.all_to_all(
+            jnp.stack(
+                jnp.split(
+                    jnp.stack([back_real, back_imag]).astype(jnp.bfloat16),
+                    lax.axis_size("mom"),
+                    axis=3,
+                )
+            ),
+            "mom",
+            0,
+            0,
+        ),
+        axis=4,
     )
     field_pts = field_pts.reshape(pair_values.shape)
     weighted = complex_mix("bnkum,kvm->bnkvu", field_pts, val_orbitals, 1.0, 1.0).astype(

time: 1020 us -> 960 us (0.941)
  local copies, waits for them, and re-layouts: 259 us -> 204 us
  blocking collectives: 252 us -> 238 us
    another operation x7, local copies, waits for them, and re-layouts: 99.8 us -> 66.6 us
    all_to_all x1 -> x0, local copies, waits for them, and re-layouts: 30.2 us -> none  [on_device(): lax.all_to_all(jnp.stack([back_real, back_imag]).astype(jnp.bfloat16), 'm...]
    another operation x1 -> x3, other arithmetic: 1.36 us -> 17.5 us  [the longest x2 16.2 us: on_device(): jnp.stack(jnp.split(jnp.stack([back_real, back_imag]).astype(jnp.bfloat16...]
    all_to_all x1, blocking collectives: 200 us -> 186 us  [on_device(): lax.all_to_all(jnp.stack(jnp.split(jnp.stack([back_real, back_imag]).asty...]
  transfers between devices with their start and end apart: 3 -> 3, of which waited for: 2 -> 2; matrix products, arithmetic and copies ran while one was open for 53% -> 51% of each run, Pallas kernels for 0% -> 0%
where the time goes in v1:
time: 960 us; the launch traced here: 948 us
  matrix products  246 us (26%)
  blocking collectives  238 us (25%)
  local copies, waits for them, and re-layouts  204 us (21%)
  waiting for transfers between devices  165 us (17%)
  other arithmetic  70.6 us (7%)
  between operations  14.1 us (1%)
  starting transfers between devices  10.2 us (1%)
    all_to_all x1, blocking collectives, on_device(): lax.all_to_all(jnp.stack(jnp.split(jnp.stack([back_real, back_imag]).asty...  186 us
    all_to_all x1, waiting for transfers between devices, on_device(): lax.all_to_all(flattened, 'mom', split_axis=4, concat_axis=3, tiled=True)  151 us
    another operation x6, local copies, waits for them, and re-layouts  59.4 us
    all_to_all x1, blocking collectives, on_device(): lax.all_to_all(weighted, 'pts', split_axis=4, concat_axis=5, tiled=True)  52 us
    another operation x3, local copies, waits for them, and re-layouts, complex_mix(): jnp.stack([real_real - left_sign * right_sign * imag_imag, right_sign * r...  40.2 us
    dot_general x4, matrix products, complex_mix(): jnp.einsum(formula, left[1], right[1], preferred_element_type=jnp.float32)  35.7 us
    dot_general x4, matrix products, complex_mix(): jnp.einsum(formula, left[1], right[0], preferred_element_type=jnp.float32)  35.5 us
    dot_general x4, matrix products, complex_mix(): jnp.einsum(formula, left[0], right[1], preferred_element_type=jnp.float32)  33.9 us
  transfers between devices with their start and end apart: 3, of which 2 were waited for; matrix products, arithmetic and copies ran while one was open for 51% of the time, Pallas kernels for 0%

profile of v1, /device:TPU:0, one launch (start us, length us, event | category | flops | bytes accessed | tf_op | source)
XLA Modules:
  0.0 948.0 jit_solution(10482630740440165149)
XLA Ops:
  7.3 4.6 fusion.137
  20.1 5.4 fusion.47
  25.5 5.4 fusion.48
  30.9 9.8 %fusion.20 = f32[128,2,32,512]{3,2,1,0:T(8,128)} fusion(bf16[2,128,64,32]{2,3,0,1:T(8,128)(2,1)} %fusion.47, bf16[2,128,64,512]{3,2,1,0:T(8,128)(2,1)S(1)} %bitcast.308), kind=kOutput, calls=%fused_computation.40 | convolution fusion | flops 536870912 | bytes 26214400 | tf_op jit(solution)/shard_map/bnkvu,kvm->bnkum/dot_general | solution.py:15
  40.8 14.0 %fusion.37 = bf16[2,1,128,32,512]{4,3,0,2,1:T(8,128)(2,1)} fusion(f32[128,2,32,512]{3,2,1,0:T(8,128)} %fusion.20, bf16[2,128,64,32]{2,3,0,1:T(8,128)(2,1)} %fusion.48, bf16[2,128,64,512]{3,2,1,0:T(8,128)(2,1)} %param.9), kind=kOutput, calls=%fused_computation.57 | convolution fusion | flops 549453824 | bytes 35651584 | tf_op jit(solution)/shard_map/bnkvu,kvm->bnkum/dot_general | solution.py:16
  54.7 16.5 %copy.232 = bf16[2,1,128,32,512]{2,0,4,3,1:T(2,128)(2,1)} copy(bf16[2,1,128,32,512]{4,3,0,2,1:T(8,128)(2,1)} %fusion.37) | data formatting | bytes 16777216 | tf_op jit(solution)/shard_map/stack | solution.py:19
  71.2 12.1 %fusion.26 = f32[128,2,32,512]{3,2,1,0:T(8,128)} fusion(bf16[2,128,64,32]{2,3,0,1:T(8,128)(2,1)S(1)} %copy-done.6, bf16[2,128,64,512]{3,2,1,0:T(8,128)(2,1)} %param.9), kind=kOutput, calls=%fused_computation.46 | convolution fusion | flops 536870912 | bytes 26214400 | tf_op jit(solution)/shard_map/bnkvu,kvm->bnkum/dot_general | solution.py:17
  83.4 12.9 %fusion.40 = bf16[2,1,128,32,512]{4,3,0,2,1:T(8,128)(2,1)} fusion(bf16[2,128,64,32]{2,3,0,1:T(8,128)(2,1)S(1)} %copy-done.4, bf16[2,128,64,512]{3,2,1,0:T(8,128)(2,1)} %param.9, f32[128,2,32,512]{3,2,1,0:T(8,128)} %fusion.26), kind=kOutput, calls=%fused_computation.58 | convolution fusion | flops 549453824 | bytes 34603008 | tf_op jit(solution)/shard_map/bnkvu,kvm->bnkum/dot_general | solution.py:18
  96.3 15.7 %copy.233 = bf16[2,1,128,32,512]{2,0,4,3,1:T(2,128)(2,1)} copy(bf16[2,1,128,32,512]{4,3,0,2,1:T(8,128)(2,1)} %fusion.40) | data formatting | bytes 16777216 | tf_op jit(solution)/shard_map/stack | solution.py:19
  112.0 26.4 %pad_maximum_fusion.1 = bf16[2,2,1,128,16384]{3,1,2,0,4:T(2,128)(2,1)} fusion(bf16[1,2,1,128,16384]{3,1,2,0,4:T(2,128)(2,1)} %bitcast.318, bf16[1,2,1,128,16384]{3,1,2,0,4:T(2,128)(2,1)} %bitcast.317), kind=kLoop, calls=%fused_computation.7 | loop fusion | flops 8388608 | bytes 33554432 | tf_op jit(solution)/shard_map/stack | solution.py:19
  138.4 9.8 %all-to-all-start = ((bf16[2,2,1,128,16384]{3,1,2,0,4:T(2,128)(2,1)}), bf16[2,2,1,128,16384]{3,1,2,0,4:T(2,128)(2,1)}, u32[]{:S(2)}, u32[]{:S(2)}) async-start(bf16[2,2,1,128,16384]{3,1,2,0,4:T(2,128)(2,1)} %pad_maximum_fusion.1), calls=%async_computation | async-start | bytes 33554432 | tf_op jit(solution)/shard_map/all_to_all | solution.py:54
  148.3 12.1 %slice_convert_fusion.1 = (f32[1,256,16,512]{3,2,1,0:T(8,128)}, f32[1,256,16,512]{3,2,1,0:T(8,128)}) fusion(bf16[2,256,16,512]{3,2,1,0:T(8,128)(2,1)} %param.11), kind=kLoop, calls=%fused_computation.67 | loop fusion | flops 4194304 | bytes 25165824 | tf_op jit(solution)/shard_map/convert_element_type | solution.py:61
  160.3 9.9 %copy.231 = f32[1,256,16,512]{1,3,2,0:T(8,128)} copy(f32[1,256,16,512]{3,2,1,0:T(8,128)} %get-tuple-element.17) | data formatting | bytes 16777216 | tf_op jit(solution)/shard_map/convert_element_type | solution.py:61
  170.2 10.0 %copy.234 = f32[1,256,16,512]{1,3,2,0:T(8,128)} copy(f32[1,256,16,512]{3,2,1,0:T(8,128)} %get-tuple-element.18) | data formatting | bytes 16777216 | tf_op jit(solution)/shard_map/convert_element_type | solution.py:61
  180.2 151.0 %all-to-all-done = bf16[2,2,1,128,16384]{3,1,2,0,4:T(2,128)(2,1)} async-done(((bf16[2,2,1,128,16384]{3,1,2,0,4:T(2,128)(2,1)}), bf16[2,2,1,128,16384]{3,1,2,0,4:T(2,128)(2,1)}, u32[]{:S(2)}, u32[]{:S(2)}) %all-to-all-start) | async-done | bytes 16777248 | tf_op jit(solution)/shard_map/all_to_all | solution.py:54
  331.2 28.1 %copy.273 = bf16[2,2,1,128,2,8192]{3,4,5,1,2,0:T(2,128)(2,1)S(1)} copy(bf16[2,2,1,128,2,8192]{3,1,0,5,4,2:T(2,128)(2,1)} %bitcast.38) | data formatting | bytes 33554432 | tf_op jit(solution)/shard_map/all_to_all | solution.py:54
  359.3 13.0 %fusion.136 = (bf16[1,2,1,2,128,8192]{4,3,5,1,2,0:T(2,128)(2,1)}, bf16[1,2,1,2,128,8192]{4,3,5,1,2,0:T(2,128)(2,1)}) fusion(bf16[2,2,1,2,128,8192]{4,3,5,1,2,0:T(2,128)(2,1)S(1)} %bitcast.313), kind=kLoop, calls=%fused_computation.185 | loop fusion | bytes 33554432 | tf_op jit(solution)/shard_map/slice | solution.py:56
  372.3 14.1 %reshape.540 = bf16[2,256,8192]{1,2,0:T(8,128)(2,1)} reshape(bf16[1,2,1,2,128,8192]{4,3,5,1,2,0:T(2,128)(2,1)} %get-tuple-element.16) | data formatting | bytes 16777216 | tf_op jit(solution)/shard_map/reshape.28
  386.4 14.2 %reshape.539 = bf16[2,256,8192]{1,2,0:T(8,128)(2,1)} reshape(bf16[1,2,1,2,128,8192]{4,3,5,1,2,0:T(2,128)(2,1)} %get-tuple-element.15) | data formatting | bytes 16777216 | tf_op jit(solution)/shard_map/reshape.24
  400.6 12.5 %fusion.94 = f32[2,8192,256]{2,1,0:T(8,128)} fusion(bf16[2,256,8192]{1,2,0:T(8,128)(2,1)} %reshape.540, s32[256]{0:T(256)S(1)} %copy-done.8), kind=kOutput, calls=%fused_computation.140 | convolution fusion | flops 2148466688 | bytes 25166848 | tf_op jit(solution)/shard_map/fs,bnsc->bnfc/dot_general | solution.py:58
  413.2 9.0 fusion.96
  422.2 14.8 %convolution_subtract_fusion = f32[2,8192,256]{2,1,0:T(8,128)} fusion(f32[2,8192,256]{2,1,0:T(8,128)} %fusion.94, bf16[2,256,8192]{1,2,0:T(8,128)(2,1)S(1)} %copy-done.1, s32[256]{0:T(256)S(1)} %copy-done.8), kind=kOutput, calls=%fused_computation.26 | convolution fusion | flops 2152660992 | bytes 41944064 | tf_op jit(solution)/shard_map/fs,bnsc->bnfc/dot_general | solution.py:60
  437.0 27.4 %fusion.11 = (bf16[2,256,8192]{1,2,0:T(8,128)(2,1)}, bf16[2,256,8192]{1,2,0:T(8,128)(2,1)}) fusion(f32[2,8192,256]{2,1,0:T(8,128)} %convolution_subtract_fusion, f32[256,8192]{0,1:T(8,128)} %bitcast.312, f32[256,8192]{0,1:T(8,128)} %bitcast.311, f32[2,8192,256]{2,1,0:T(8,128)} %fusion.96, bf16[2,256,8192]{1,2,0:T(8,128)(2,1)} %reshape.540, s32[256]{0:T(256)S(1)} %copy-done.8), kind=kOutput, calls=%fused_computation.30 | convolution fusion | flops 2186215424 | bytes 75498496 | tf_op jit(solution)/shard_map/fs,bnsc->bnfc/dot_general | solution.py:57
  464.4 12.5 %fusion.90 = f32[2,8192,256]{2,1,0:T(8,128)} fusion(bf16[2,256,8192]{1,2,0:T(8,128)(2,1)} %get-tuple-element.11, s32[256]{0:T(256)S(1)} %copy-done.8), kind=kOutput, calls=%fused_computation.138 | convolution fusion | flops 2148466688 | bytes 25166848 | tf_op jit(solution)/shard_map/fs,bnfc->bnsc/dot_general | solution.py:68
  477.0 9.0 fusion.92
  486.0 13.5 %fusion.10 = bf16[1,2,1,256,8192]{3,4,1,2,0:T(8,128)(2,1)} fusion(f32[2,8192,256]{2,1,0:T(8,128)} %fusion.90, bf16[2,256,8192]{1,2,0:T(8,128)(2,1)} %get-tuple-element.12, s32[256]{0:T(256)S(1)} %copy-done.8), kind=kOutput, calls=%fused_computation.29 | convolution fusion | flops 2161049600 | bytes 33555456 | tf_op jit(solution)/shard_map/fs,bnfc->bnsc/dot_general | solution.py:69
  499.5 11.2 %fusion.9 = bf16[1,2,1,256,8192]{3,4,1,2,0:T(8,128)(2,1)} fusion(f32[2,8192,256]{2,1,0:T(8,128)} %fusion.92, bf16[2,256,8192]{1,2,0:T(8,128)(2,1)S(1)} %bitcast.310, s32[256]{0:T(256)S(1)} %copy-done.8), kind=kOutput, calls=%fused_computation.28 | convolution fusion | flops 2161049600 | bytes 33555456 | tf_op jit(solution)/shard_map/fs,bnfc->bnsc/dot_general | solution.py:65
  510.7 8.1 fusion.14
  522.1 6.7 fusion
  528.8 7.2 slice_bitcast_fusion.6
  535.9 8.0 pad_maximum_fusion.2
  543.9 185.8 %all_to_all.35 = bf16[2,2,2,1,128,8192]{4,5,2,1,3,0:T(8,128)(2,1)S(1)} all-to-all(bf16[2,2,2,1,128,8192]{4,5,2,1,3,0:T(8,128)(2,1)S(1)} %pad_maximum_fusion.2), channel_id=1, replica_groups=mesh['mom'=2,'pts'=16] {'mom'}, dimensions={0} | all-to-all | bytes 33554432 | tf_op jit(solution)/shard_map/all_to_all | solution.py:72
  729.8 6.0 fusion.135
  735.8 7.2 copy.200
  743.0 14.7 %copy.201 = bf16[2,128,32,512]{3,2,0,1:T(8,128)(2,1)} copy(bf16[2,128,32,512]{1,3,2,0:T(8,128)(2,1)} %bitcast.315) | data formatting | bytes 16777216 | tf_op jit(solution)/shard_map/reshape.49
  757.7 7.2 copy.202
  764.9 14.7 %copy.203 = bf16[2,128,32,512]{3,2,0,1:T(8,128)(2,1)} copy(bf16[2,128,32,512]{1,3,2,0:T(8,128)(2,1)} %bitcast.316) | data formatting | bytes 16777216 | tf_op jit(solution)/shard_map/reshape.53
  779.5 10.1 %fusion.17 = f32[128,2,32,64]{3,2,1,0:T(8,128)} fusion(bf16[2,128,32,512]{3,2,0,1:T(8,128)(2,1)} %copy.201, bf16[2,128,64,512]{3,2,1,0:T(8,128)(2,1)} %param.9), kind=kOutput, calls=%fused_computation.37 | convolution fusion | flops 536870912 | bytes 18874368 | tf_op jit(solution)/shard_map/bnkum,kvm->bnkvu/dot_general | solution.py:15
  789.6 10.1 %fusion.15 = f32[128,2,32,64]{3,2,1,0:T(8,128)} fusion(bf16[2,128,32,512]{3,2,0,1:T(8,128)(2,1)} %copy.203, bf16[2,128,64,512]{3,2,1,0:T(8,128)(2,1)} %param.9), kind=kOutput, calls=%fused_computation.35 | convolution fusion | flops 536870912 | bytes 18874368 | tf_op jit(solution)/shard_map/bnkum,kvm->bnkvu/dot_general | solution.py:18
  799.7 9.3 fusion.49
  809.0 10.7 %fusion.50 = bf16[1,2,1,128,64,32]{4,5,1,3,2,0:T(8,128)(2,1)} fusion(f32[128,2,32,64]{3,2,1,0:T(8,128)} %fusion.15, bf16[2,128,32,512]{3,2,0,1:T(8,128)(2,1)} %copy.201, bf16[2,128,64,512]{3,2,1,0:T(8,128)(2,1)} %param.9), kind=kOutput, calls=%fused_computation.75 | convolution fusion | flops 537919488 | bytes 22020096 | tf_op jit(solution)/shard_map/bnkum,kvm->bnkvu/dot_general | solution.py:17
  824.3 8.0 copy.206
  832.3 52.0 %all_to_all.36 = bf16[2,2,1,128,64,32]{3,5,2,1,0,4:T(8,128)(2,1)S(1)} all-to-all(bf16[2,2,1,128,64,32]{3,5,2,1,0,4:T(8,128)(2,1)S(1)} %copy.206), channel_id=1, replica_groups=mesh['mom'=2,'pts'=16] {'pts'}, dimensions={4} | all-to-all | bytes 4194304 | tf_op jit(solution)/shard_map/all_to_all | solution.py:90
  889.4 7.0 fusion.6
  896.5 7.1 fusion.7
  903.5 7.0 fusion.5
  910.6 7.1 fusion.8
  921.1 12.8 %collective-permute-done = bf16[2,2,1,128,4,128]{5,3,4,2,1,0:T(8,128)(2,1)S(1)} collective-permute-done((bf16[2,2,1,128,4,128]{5,3,4,2,1,0:T(8,128)(2,1)S(1)}, bf16[2,2,1,128,4,128]{5,3,4,2,1,0:T(8,128)(2,1)S(1)}, u32[]{:S(2)}, u32[]{:S(2)}) %collective-permute-start) | collective-permute-done | bytes 524320 | tf_op jit(solution)/shard_map/ppermute | solution.py:11
  (65 shorter events, 31.9 us)
Async XLA Ops:
  6.5 882.9 %all-gather.2.cloned.1.call-start = ((), (), s32[]{:S(2)}) async-start(), calls=%async_computation.3 | async-start | bytes 35651584 | tf_op jit(solution)/shard_map/all_gather | solution.py:94
  7.3 4.6 copy-start.5
  16.0 14.9 %slice-start = ((s8[16777216]{0:T(1024)(128)(4,1)}), s8[4194304]{0:T(1024)(128)(4,1)S(1)}, s32[]{:S(2)}) async-start(s8[16777216]{0:T(1024)(128)(4,1)} %bitcast.307), calls=%async_computation.4 | async-start | bytes 8388608
  16.0 14.9 %slice-start.1 = ((s8[16777216]{0:T(1024)(128)(4,1)}), s8[4194304]{0:T(1024)(128)(4,1)S(1)}, s32[]{:S(2)}) async-start(s8[16777216]{0:T(1024)(128)(4,1)} %bitcast.307), calls=%async_computation.5 | async-start | bytes 8388608
  20.0 10.9 %slice-start.2 = ((s8[16777216]{0:T(1024)(128)(4,1)}), s8[4194304]{0:T(1024)(128)(4,1)S(1)}, s32[]{:S(2)}) async-start(s8[16777216]{0:T(1024)(128)(4,1)} %bitcast.307), calls=%async_computation.6 | async-start | bytes 8388608
  25.5 5.4 slice-start.3
  54.7 16.5 %copy-start.6 = (bf16[2,128,64,32]{2,3,0,1:T(8,128)(2,1)S(1)}, bf16[2,128,64,32]{2,3,0,1:T(8,128)(2,1)}, u32[]{:S(2)}) copy-start(bf16[2,128,64,32]{2,3,0,1:T(8,128)(2,1)} %fusion.47) | copy-start | bytes 3145732
  71.2 12.1 %copy-start.4 = (bf16[2,128,64,32]{2,3,0,1:T(8,128)(2,1)S(1)}, bf16[2,128,64,32]{2,3,0,1:T(8,128)(2,1)}, u32[]{:S(2)}) copy-start(bf16[2,128,64,32]{2,3,0,1:T(8,128)(2,1)} %fusion.48) | copy-start | bytes 3145732
  138.4 192.8 %all-to-all-start = ((bf16[2,2,1,128,16384]{3,1,2,0,4:T(2,128)(2,1)}), bf16[2,2,1,128,16384]{3,1,2,0,4:T(2,128)(2,1)}, u32[]{:S(2)}, u32[]{:S(2)}) async-start(bf16[2,2,1,128,16384]{3,1,2,0,4:T(2,128)(2,1)} %pad_maximum_fusion.1), calls=%async_computation | async-start | bytes 33554432 | tf_op jit(solution)/shard_map/all_to_all | solution.py:54
  386.4 14.2 %copy-start.8 = (s32[256]{0:T(256)S(1)}, s32[256]{0:T(256)}, u32[]{:S(2)}) copy-start(s32[256]{0:T(256)} %param.14) | copy-start | bytes 3076
  400.6 12.6 %copy-start.1 = (bf16[2,256,8192]{1,2,0:T(8,128)(2,1)S(1)}, bf16[2,256,8192]{1,2,0:T(8,128)(2,1)}, u32[]{:S(2)}) copy-start(bf16[2,256,8192]{1,2,0:T(8,128)(2,1)} %reshape.539) | copy-start | bytes 25165828
  464.4 12.6 %copy-start = (bf16[2,256,8192]{1,2,0:T(8,128)(2,1)S(1)}, bf16[2,256,8192]{1,2,0:T(8,128)(2,1)}, u32[]{:S(2)}) copy-start(bf16[2,256,8192]{1,2,0:T(8,128)(2,1)} %get-tuple-element.12) | copy-start | bytes 25165828
  464.4 35.1 %slice-start.4 = ((s8[8388608]{0:T(1024)(128)(4,1)}), s8[4194304]{0:T(1024)(128)(4,1)S(1)}, s32[]{:S(2)}) async-start(s8[8388608]{0:T(1024)(128)(4,1)} %bitcast.309), calls=%async_computation.8 | async-start | bytes 8388608
  477.0 22.6 %slice-start.5 = ((s8[8388608]{0:T(1024)(128)(4,1)}), s8[4194304]{0:T(1024)(128)(4,1)S(1)}, s32[]{:S(2)}) async-start(s8[8388608]{0:T(1024)(128)(4,1)} %bitcast.309), calls=%async_computation.9 | async-start | bytes 8388608
  510.7 8.4 copy-start.2
  510.7 11.3 %copy-start.3 = (bf16[1,2,1,256,8192]{3,4,1,2,0:T(8,128)(2,1)S(1)}, bf16[1,2,1,256,8192]{3,4,1,2,0:T(8,128)(2,1)}, u32[]{:S(2)}) copy-start(bf16[1,2,1,256,8192]{3,4,1,2,0:T(8,128)(2,1)} %fusion.9) | copy-start | bytes 25165828
  910.6 8.9 copy-start.10
  917.6 18.9 %copy-start.7 = (f32[128,128]{1,0:T(8,128)S(1)}, f32[128,128]{1,0:T(8,128)}, u32[]{:S(2)}) copy-start(f32[128,128]{1,0:T(8,128)} %param.13) | copy-start | bytes 196612
  917.7 18.9 %copy-start.9 = (f32[128,4]{0,1:T(4,128)S(1)}, f32[128,4]{0,1:T(4,128)}, u32[]{:S(2)}) copy-start(f32[128,4]{0,1:T(4,128)} %param.12) | copy-start | bytes 6148
  919.1 14.9 %collective-permute-start = (bf16[2,2,1,128,4,128]{5,3,4,2,1,0:T(8,128)(2,1)S(1)}, bf16[2,2,1,128,4,128]{5,3,4,2,1,0:T(8,128)(2,1)S(1)}, u32[]{:S(2)}, u32[]{:S(2)}) collective-permute-start(bf16[2,2,1,128,4,128]{5,3,4,2,1,0:T(8,128)(2,1)S(1)} %pad_maximum_fusion.5), channel_id=1, source_target_pairs={{0,16},{16,0},{1,17},{17,1},{2,18},{18,2},{3,19},{19,3},{4,20},{20... | collective-permute-start | bytes 1572872 | tf_op jit(solution)/shard_map/ppermute | solution.py:11
Sparse Core Ops, SparseCore 0:
  8.9 170.7 all-gather.1
